TPU v7x, 256 devices: a whole 4x4x8 slice. The times are simulated.
256 devices in a mesh: grp: 8 (over z), tp: 32 (over x, y, core).
Axes of the slice: x: 4, y: 4, z: 8, core: 2. Of those that a mesh axis runs over, the one named last changes fastest.
Arguments:
- hidden_in: bfloat16 [1024, 3584], P(('grp', 'tp')), may hold values from -6 to 6
- norm_gains: float32 [4, 3584], replicated, may hold values from 0.25 to 1.75
- w_qkv: bfloat16 [3584, 8192], P(None, 'tp'), may hold values from -0.09375 to 0.09375
- w_out: bfloat16 [4096, 3584], P('tp'), may hold values from -0.09375 to 0.09375
- w_gate_up: bfloat16 [2, 3584, 8192], P(None, None, 'tp'), may hold values from -0.09375 to 0.09375
- w_down: bfloat16 [8192, 3584], P('tp'), may hold values from -0.0625 to 0.0625
- prompt_keys: bfloat16 [32768, 2048], P(('grp', 'tp')), may hold values from -480 to 480, as said below
- prompt_values: bfloat16 [32768, 2048], P(('grp', 'tp')), may hold values from -6 to 6
- tail_keys: bfloat16 [1024, 64, 2048], P(('grp', 'tp')), may hold values from -480 to 480, as said below
- tail_values: bfloat16 [1024, 64, 2048], P(('grp', 'tp')), may hold values from -6 to 6
- prompt_len: int32 [80], replicated, may hold values from 1 to 4087, as said below
- group_home: int32 [80], replicated, may hold values from 0 to 7, as said below
- req_group: int32 [1024], P('grp'), may hold values from 0 to 79, as said below
- tail_len: int32 [1024], P('grp'), may hold values from 1 to 64, 32768 in all
Outputs:
- layer_out: bfloat16 [1024, 3584], P(('grp', 'tp'))
Inputs may be any that keep to these rules, and one draw needn't show every extreme that they name: `group_home`: each grp device is home to exactly 10 groups. `prompt_len`: the prompts of the groups homed on one grp device lie one after another in order of group id from the first of that device's 4096 cache positions; together they hold at most 4096 positions, exactly 4096 on one home in every draw, where one group holds 4087 of them. `req_group`: of the 128 requests held by one grp device, at most 32 belong to groups homed on any one grp device; in every draw one home receives exactly 32 requests from every grp device. `prompt_keys`: cached keys, already rotated. `tail_keys`: cached keys, already rotated.
All inputs are finite; a program needn't handle non-finite values. No bound on the sum of `tail_len` on one device may be relied on, other than what follows from the above.
Results may differ from a plain program's by a relative error of at most 0.015.
Values may be sent and summed in bfloat16 or wider, within the bound.
A program may use at most 128 MiB of HBM per device.

v0:
```python
import math
import jax
import jax.numpy as jnp
from jax import lax
from jax.sharding import PartitionSpec as P

HEADS = 16
KV_HEADS = 8
HEAD_DIM = 256
NORM_EPS = 1e-06
SOFT_CAP = 50.0


def rms_scale(values, gain_row):
    values = values.astype(jnp.float32)
    return (
        values * lax.rsqrt(jnp.mean(values * values, axis=-1, keepdims=True) + NORM_EPS) * gain_row
    )


def rotate(head_rows, position):
    half_width = head_rows.shape[-1] // 2
    freq_index = jnp.arange(half_width).astype(jnp.float32)
    frequency = jnp.exp(freq_index * (-math.log(10000.0) / half_width))
    angles = position.astype(jnp.float32)[:, None] * frequency[None, :]
    cosine = jnp.cos(angles)[:, None, :]
    sine_part = jnp.sin(angles)[:, None, :]
    head_rows = head_rows.astype(jnp.float32)
    first_half = head_rows[..., :half_width]
    second = head_rows[..., half_width:]
    return jnp.concatenate(
        [first_half * cosine - second * sine_part, second * cosine + first_half * sine_part],
        axis=-1,
    )


def capped(scores):
    return SOFT_CAP * jnp.tanh(scores * HEAD_DIM ** (-0.5) / SOFT_CAP)


def lookup(lookup_table, index_list):
    matches = index_list[:, None] == jnp.arange(lookup_table.shape[0], dtype=jnp.int32)[None, :]
    return jnp.sum(jnp.where(matches, lookup_table[None, :], 0), axis=1)


def group_starts(prompt_len, group_home):
    group_ids = jnp.arange(prompt_len.shape[0], dtype=jnp.int32)
    same_home = group_home[:, None] == group_home[None, :]
    earlier = group_ids[None, :] < group_ids[:, None]
    return jnp.sum(jnp.where(same_home & earlier, prompt_len[None, :], 0), axis=1)


def shared_part(queries, key_rows, value_rows, visible):
    scores = capped(
        jnp.einsum("nkjd,pkd->nkjp", queries, key_rows, preferred_element_type=jnp.float32)
    )
    exponent = jnp.where(visible[:, None, None, :], jnp.exp(scores), 0.0)
    numerator = jnp.einsum(
        "nkjp,pkd->nkjd",
        exponent.astype(jnp.bfloat16),
        value_rows,
        preferred_element_type=jnp.float32,
    )
    return (numerator, jnp.sum(exponent, axis=-1))


def own_part(queries, key_rows, value_rows, visible):
    scores = capped(
        jnp.einsum("nkjd,npkd->nkjp", queries, key_rows, preferred_element_type=jnp.float32)
    )
    exponent = jnp.where(visible[:, None, None, :], jnp.exp(scores), 0.0)
    numerator = jnp.einsum(
        "nkjp,npkd->nkjd",
        exponent.astype(jnp.bfloat16),
        value_rows,
        preferred_element_type=jnp.float32,
    )
    return (numerator, jnp.sum(exponent, axis=-1))


def per_device(
    hidden_in,
    norm_gains,
    w_qkv,
    w_out,
    w_gate_up,
    w_down,
    prompt_keys,
    prompt_values,
    tail_keys,
    tail_values,
    prompt_len,
    group_home,
    req_group,
    tail_len,
):
    tp_rank = lax.axis_index("tp")
    q_width = HEADS * HEAD_DIM
    kv_width = KV_HEADS * HEAD_DIM
    row_count = hidden_in.shape[0]
    normed = rms_scale(hidden_in, norm_gains[0]).astype(jnp.bfloat16)
    qkv_share = jnp.dot(
        lax.all_gather(normed, "tp", axis=0, tiled=True), w_qkv, preferred_element_type=jnp.float32
    ).astype(jnp.bfloat16)
    projected_qkv = lax.all_gather(qkv_share, "tp", axis=1, tiled=True)
    requests = projected_qkv.shape[0]
    req_len = lookup(prompt_len, req_group)
    position = req_len + tail_len
    queries = rotate(
        projected_qkv[:, :q_width].reshape(requests, HEADS, HEAD_DIM), position
    ).astype(jnp.bfloat16)
    queries = queries.reshape(requests, KV_HEADS, 2, HEAD_DIM)
    key_new = rotate(
        projected_qkv[:, q_width : q_width + kv_width].reshape(requests, KV_HEADS, HEAD_DIM),
        position,
    ).astype(jnp.bfloat16)
    value_new = projected_qkv[:, q_width + kv_width :].reshape(requests, KV_HEADS, HEAD_DIM)
    starts = group_starts(prompt_len, group_home)
    req_home = lookup(group_home, req_group)
    req_start = lookup(starts, req_group)
    cap_dev = prompt_keys.shape[0]
    row_first = tp_rank * row_count
    own_queries = lax.dynamic_slice_in_dim(queries, row_first, row_count, 0)
    own_tail_len = lax.dynamic_slice_in_dim(tail_len, row_first, row_count, 0)
    tail_dev = tail_keys.shape[1]
    tail_pos = jnp.arange(tail_dev, dtype=jnp.int32)
    own_num, own_den = own_part(
        own_queries,
        tail_keys.reshape(row_count, tail_dev, KV_HEADS, HEAD_DIM),
        tail_values.reshape(row_count, tail_dev, KV_HEADS, HEAD_DIM),
        tail_pos[None, :] < own_tail_len[:, None],
    )
    numerator = lax.dynamic_update_slice_in_dim(
        jnp.zeros((requests, KV_HEADS, 2, HEAD_DIM), jnp.float32), own_num, row_first, 0
    )
    denominator = lax.dynamic_update_slice_in_dim(
        jnp.zeros((requests, KV_HEADS, 2), jnp.float32), own_den, row_first, 0
    )
    key_piece = lax.all_gather(prompt_keys, "grp", axis=0, tiled=True)
    value_piece = lax.all_gather(prompt_values, "grp", axis=0, tiled=True)
    piece_rows = key_piece.shape[0]
    gathered_index = jnp.arange(piece_rows, dtype=jnp.int32)
    home_index = gathered_index // cap_dev
    piece_offsets = tp_rank * cap_dev + gathered_index % cap_dev
    visible = (
        (home_index[None, :] == req_home[:, None])
        & (piece_offsets[None, :] >= req_start[:, None])
        & (piece_offsets[None, :] < (req_start + req_len)[:, None])
    )
    part_num, part_den = shared_part(
        queries,
        key_piece.reshape(piece_rows, KV_HEADS, HEAD_DIM),
        value_piece.reshape(piece_rows, KV_HEADS, HEAD_DIM),
        visible,
    )
    numerator, denominator = (numerator + part_num, denominator + part_den)
    share_width = w_out.shape[0]
    first_col = tp_rank * share_width
    flat_num = numerator.reshape(requests, q_width)
    flat_den = denominator.reshape(requests, HEADS)
    total_num, total_den = lax.psum((flat_num, flat_den), "tp")
    share_num = lax.dynamic_slice_in_dim(total_num, first_col, share_width, 1)
    self_exp = jnp.exp(
        capped(jnp.einsum("nkjd,nkd->nkj", queries, key_new, preferred_element_type=jnp.float32))
    )
    self_num = (
        lax.optimization_barrier(self_exp.astype(jnp.bfloat16)).astype(jnp.float32)[..., None]
        * value_new.astype(jnp.float32)[:, :, None, :]
    )
    self_share = lax.dynamic_slice_in_dim(
        self_num.reshape(requests, q_width), first_col, share_width, 1
    )
    total_den = total_den + self_exp.reshape(requests, HEADS)
    head_of_col = (first_col + jnp.arange(share_width, dtype=jnp.int32)) // HEAD_DIM
    head_pick = (head_of_col[None, :] == jnp.arange(HEADS, dtype=jnp.int32)[:, None]).astype(
        jnp.float32
    )
    den_cols = jnp.dot(total_den, head_pick, precision=lax.Precision.HIGHEST)
    attn_share = ((share_num + self_share) / den_cols).astype(jnp.bfloat16)
    block_rows = attn_share
    attn_proj = lax.psum_scatter(
        jnp.dot(block_rows, w_out, preferred_element_type=jnp.float32),
        "tp",
        scatter_dimension=0,
        tiled=True,
    )
    resid = (hidden_in.astype(jnp.float32) + rms_scale(attn_proj, norm_gains[1])).astype(
        jnp.bfloat16
    )
    ffn_in = rms_scale(resid, norm_gains[2]).astype(jnp.bfloat16)
    gate_up = jnp.einsum(
        "rd,kdf->krf",
        lax.all_gather(ffn_in, "tp", axis=0, tiled=True),
        w_gate_up,
        preferred_element_type=jnp.float32,
    )
    hidden_units = (jax.nn.gelu(gate_up[0], approximate=True) * gate_up[1]).astype(jnp.bfloat16)
    block_rows = hidden_units
    ffn_proj = lax.psum_scatter(
        jnp.dot(block_rows, w_down, preferred_element_type=jnp.float32).astype(jnp.bfloat16),
        "tp",
        scatter_dimension=0,
        tiled=True,
    ).astype(jnp.float32)
    return (resid.astype(jnp.float32) + rms_scale(ffn_proj, norm_gains[3])).astype(jnp.bfloat16)


def solution(mesh):
    in_specs = (
        P(("grp", "tp"), None),
        P(),
        P(None, "tp"),
        P("tp", None),
        P(None, None, "tp"),
        P("tp", None),
        P(("grp", "tp"), None),
        P(("grp", "tp"), None),
        P(("grp", "tp"), None, None),
        P(("grp", "tp"), None, None),
        P(),
        P(),
        P("grp"),
        P("grp"),
    )
    out_specs = P(("grp", "tp"), None)
    return jax.shard_map(
        per_device, mesh=mesh, in_specs=in_specs, out_specs=out_specs, check_vma=False
    )
```

profile of v0, /device:TPU:1, one launch (start us, length us, event | category | flops | bytes accessed | tf_op | source)
XLA Modules:
  0.0 625.6 jit_solution(4266515688802575155)
XLA Ops:
  6.5 1.2 slice_reduce_fusion.1
  7.7 0.9 fusion.35
  8.6 0.8 fusion.47
  9.5 26.6 %all-gather = bf16[32,4,3584]{2,1,0:T(4,128)(2,1)S(1)} all-gather(bf16[1,4,3584]{2,1,0:T(4,128)(2,1)S(1)} %fusion.47), channel_id=1, replica_groups=mesh['grp'=8,'tp'=32] {'tp'}, dimensions={0}, use_global_device_ids=true | all-gather | bytes 946176 | tf_op jit(solution)/shard_map/all_gather | solution.py:103
  36.0 1.1 reshape.279
  37.2 2.9 convolution_convert_fusion.1
  40.1 1.0 copy.77
  41.2 1.0 copy.79
  42.3 0.0 all-reduce.6.cloned.1.call-start
  42.3 0.1 dynamic_slice.12
  42.5 0.2 select_reduce_fusion.2
  42.6 0.1 select_reduce_fusion.3
  42.8 0.1 iota_compare_fusion.4
  42.8 0.3 multiply_cosine_fusion
  43.1 0.9 compare_and_fusion
  44.0 46.5 %all-gather.6.cloned.1.call-done = bf16[128,8192]{1,0:T(8,128)(2,1)} async-done(((bf16[128,256]{1,0:T(8,128)(2,1)}), bf16[128,8192]{1,0:T(8,128)(2,1)}) %all-gather.6.cloned.1.call-update) | async-done | bytes 2097168 | tf_op jit(solution)/shard_map/all_gather | solution.py:105
  90.5 1.4 slice_convert_fusion
  91.9 0.7 copy.101
  92.6 0.3 subtract_convert_fusion
  92.9 0.1 copy.75
  93.1 0.1 copy.76
  93.2 0.9 copy-done.11
  94.1 0.5 fusion.73
  94.6 0.1 copy.88
  94.7 2.4 slice_convert_fusion.2
  97.2 0.3 copy.102
  97.5 0.1 subtract_convert_fusion.1
  97.7 0.1 maximum_bitcast_fusion
  97.8 1.2 pad_maximum_fusion
  98.9 0.3 fusion.10
  99.2 50.9 %all-gather.8.cloned.1.call-done = bf16[1024,2048]{0,1:T(8,128)(2,1)} async-done(((bf16[128,2048]{0,1:T(8,128)(2,1)}), bf16[1024,2048]{0,1:T(8,128)(2,1)}) %all-gather.8.cloned.1.call-update) | async-done | bytes 4194320 | tf_op jit(solution)/shard_map/all_gather | solution.py:139
  150.1 7.7 %bitcast_reduce_fusion = (f32[128,8,2]{0,2,1:T(2,128)S(1)}, f32[8,128,2,1024]{3,1,2,0:T(8,128)}) fusion(pred[128,1024]{1,0:T(8,128)(4,1)} %compare_and_fusion, bf16[1024,8,256,1]{0,2,3,1:T(8,128)(2,1)} %bitcast.96, bf16[128,8,2,128]{3,0,2,1:T(8,128)(2,1)S(1)} %bitcast.87, bf16[128,8,2,128]{3,0,2,1:T(8,128)(2,1)S(1)} %bitcast.84), kind=kOutput, calls=%fused_computation | convolution fusion | flops 1084225536 | bytes 13770752 | tf_op jit(solution)/shard_map/nkjd,pkd->nkjp/dot_general | solution.py:55
  157.8 55.1 %all-gather.10.cloned.1.call-done = bf16[1024,2048]{0,1:T(8,128)(2,1)} async-done(((bf16[128,2048]{0,1:T(8,128)(2,1)}), bf16[1024,2048]{0,1:T(8,128)(2,1)}) %all-gather.10.cloned.1.call-update) | async-done | bytes 4194320 | tf_op jit(solution)/shard_map/all_gather | solution.py:140
  212.9 7.0 %fusion = f32[8,128,2,256]{3,1,2,0:T(8,128)S(1)} fusion(bf16[1024,8,256,1]{0,2,3,1:T(8,128)(2,1)} %bitcast.97, f32[8,128,2,1024]{3,1,2,0:T(8,128)} %get-tuple-element.27, pred[128,1024]{1,0:T(8,128)(4,1)} %compare_and_fusion), kind=kOutput, calls=%fused_computation.4 | convolution fusion | flops 1082130432 | bytes 14811136 | tf_op jit(solution)/shard_map/nkjp,pkd->nkjd/dot_general | solution.py:58
  220.0 1.4 copy.123
  221.3 0.7 fusion.28
  222.0 2.9 copy.85
  224.9 2.9 copy.86
  227.8 0.2 all-reduce.8.cloned.1.call-start
  228.1 3.4 fusion.15
  231.4 1.2 copy.94
  232.7 0.2 copy.87
  232.9 0.3 copy.103
  233.3 2.8 broadcast_multiply_fusion
  236.1 4.0 mul.269
  240.1 0.1 dynamic-slice_add_fusion
  240.2 1.3 add.147
  241.4 67.5 %psum.15 = f32[128,16]{0,1:T(8,128)S(1)} all-reduce(f32[128,16]{0,1:T(8,128)S(1)} %bitcast.94), channel_id=1, replica_groups=mesh['grp'=8,'tp'=32] {'tp'}, use_global_device_ids=true, to_apply=%region_8.9 | all-reduce | flops 2048 | bytes 16384 | tf_op jit(solution)/shard_map/psum | solution.py:161
  309.0 38.9 %all-reduce.6.cloned.1.call-done = f32[128,4096]{1,0:T(8,128)} async-done(((f32[128,4096]{1,0:T(8,128)}), f32[128,4096]{1,0:T(8,128)}) %all-reduce.6.cloned.1.call-update) | async-done | bytes 2097168 | tf_op jit(solution)/shard_map/psum | solution.py:161
  347.9 1.1 fusion.5
  349.1 1.6 fusion.74
  350.7 0.0 all-reduce.10.cloned.1.call-start
  350.8 0.6 dynamic-slice.6
  352.0 115.3 %all-reduce.8.cloned.1.call-done = f32[128,3584]{1,0:T(8,128)} async-done(((f32[128,3584]{1,0:T(8,128)}), f32[128,3584]{1,0:T(8,128)}) %all-reduce.8.cloned.1.call-update) | async-done | bytes 1835024
  467.4 1.0 multiply_reduce_fusion
  468.4 1.1 fusion.39
  469.5 0.1 fusion.46
  469.6 28.2 %all-gather.1 = bf16[32,4,3584]{2,1,0:T(4,128)(2,1)} all-gather(bf16[1,4,3584]{2,1,0:T(4,128)(2,1)S(1)} %fusion.46), channel_id=1, replica_groups=mesh['grp'=8,'tp'=32] {'tp'}, dimensions={0}, use_global_device_ids=true | all-gather | bytes 946176 | tf_op jit(solution)/shard_map/all_gather | solution.py:193
  497.9 1.7 reshape.286
  499.5 2.7 convolution_bitcast_fusion
  502.2 1.4 convolution_convert_fusion
  503.7 112.7 %all-reduce.10.cloned.1.call-done = bf16[128,3584]{1,0:T(8,128)(2,1)} async-done(((bf16[128,3584]{1,0:T(8,128)(2,1)}), bf16[128,3584]{1,0:T(8,128)(2,1)}) %all-reduce.10.cloned.1.call-update) | async-done | bytes 917520
  616.3 1.0 fusion.33
  617.3 1.5 fusion.42
  (45 shorter events, 0.4 us)
Async XLA Ops:
  6.5 495.7 %copy-start = (bf16[256,3584]{1,0:T(8,128)(2,1)S(1)}, bf16[256,3584]{1,0:T(8,128)(2,1)}, u32[]{:S(2)}) copy-start(bf16[256,3584]{1,0:T(8,128)(2,1)} %param.19) | copy-start | bytes 5505028
  6.5 83.9 %all-gather.6.cloned.1.call-start = ((), (), s32[]{:S(2)}) async-start(), calls=%async_computation | async-start | bytes 2162688 | tf_op jit(solution)/shard_map/all_gather | solution.py:105
  36.0 4.1 copy-start.4
  37.2 4.0 copy-start.5
  40.0 2.3 copy-start.10
  40.1 2.4 copy-start.7
  40.1 2.4 copy-start.8
  40.1 2.6 copy-start.9
  40.1 110.0 %all-gather.8.cloned.1.call-start = ((), (), s32[]{:S(2)}) async-start(), calls=%async_computation.1 | async-start | bytes 4718592 | tf_op jit(solution)/shard_map/all_gather | solution.py:139
  41.2 171.8 %all-gather.10.cloned.1.call-start = ((), (), s32[]{:S(2)}) async-start(), calls=%async_computation.2 | async-start | bytes 4718592 | tf_op jit(solution)/shard_map/all_gather | solution.py:140
  42.3 305.7 %all-reduce.6.cloned.1.call-start = ((), (), s32[]{:S(2)}) async-start(), calls=%async_computation.3 | async-start | bytes 4194304 | tf_op jit(solution)/shard_map/psum | solution.py:161
  92.9 1.2 copy-start.11
  97.5 1.4 copy-start.2
  227.8 5.1 copy-start.1
  227.8 239.5 %all-reduce.8.cloned.1.call-start = ((), (), s32[]{:S(2)}) async-start(), calls=%async_computation.4 | async-start | bytes 3670016
  236.1 113.0 %copy-start.3 = (bf16[128,3584]{1,0:T(8,128)(2,1)S(1)}, bf16[128,3584]{1,0:T(8,128)(2,1)}, u32[]{:S(2)}) copy-start(bf16[128,3584]{1,0:T(8,128)(2,1)} %param.17) | copy-start | bytes 2752516
  349.1 1.7 copy-start.12
  349.1 119.3 %copy-start.6 = (bf16[4,3584]{1,0:T(4,128)(2,1)S(1)}, bf16[4,3584]{1,0:T(4,128)(2,1)}, u32[]{:S(2)}) copy-start(bf16[4,3584]{1,0:T(4,128)(2,1)} %param.14) | copy-start | bytes 86020
  350.7 265.6 %all-reduce.10.cloned.1.call-start = ((), (), s32[]{:S(2)}) async-start(), calls=%async_computation.5 | async-start | bytes 1835008
Sparse Core Ops, SparseCore 0:
  40.2 50.2 all-gather.5
  92.2 57.8 all-gather.7
  151.8 61.1 all-gather.9
  228.0 119.9 all-reduce.5
  351.1 116.2 all-reduce.7
  503.8 112.4 all-reduce.9
where the time goes:
time: 626 us
  waiting for transfers between devices  419 us (67%)
  blocking collectives  122 us (19%)
  matrix products  28.5 us (5%)
  local copies, waits for them, and re-layouts  23.3 us (4%)
  other arithmetic  17.2 us (3%)
  between operations  14.4 us (2%)
    unnamed x8, waiting for transfers between devices  228 us
    psum x1, blocking collectives, per_device(): total_num, total_den = lax.psum((flat_num, flat_den), 'tp')  67.5 us
    all_gather x1, waiting for transfers between devices, per_device(): value_piece = lax.all_gather(prompt_values, 'grp', axis=0, tiled=True)  55.1 us
    all_gather x1, waiting for transfers between devices, per_device(): key_piece = lax.all_gather(prompt_keys, 'grp', axis=0, tiled=True)  50.9 us
    all_gather x1, waiting for transfers between devices, per_device(): projected_qkv = lax.all_gather(qkv_share, 'tp', axis=1, tiled=True)  46.5 us
    psum x1, waiting for transfers between devices, per_device(): total_num, total_den = lax.psum((flat_num, flat_den), 'tp')  38.9 us
    all_gather x1, blocking collectives, per_device(): lax.all_gather(ffn_in, 'tp', axis=0, tiled=True)  28.2 us
    all_gather x1, blocking collectives, per_device(): lax.all_gather(normed, 'tp', axis=0, tiled=True)  26.6 us
  transfers between devices with their start and end apart: 6, of which 6 were waited for; matrix products, arithmetic and copies ran while one was open for 5% of the time, Pallas kernels for 0%

commit v1 on v0

--- a/solution.py
+++ b/solution.py
@@ -9,6 +9,17 @@
 HEAD_DIM = 256
 NORM_EPS = 1e-06
 SOFT_CAP = 50.0
+
+
+def _change_levels_all(base_x, which_axis):
+    e_now = jax.lax.all_to_all(
+        jnp.stack([base_x] * jax.lax.axis_size(which_axis)),
+        concat_axis=0,
+        axis_name=which_axis,
+        split_axis=0,
+    )
+    y_new = jnp.concatenate(e_now, axis=0)
+    return y_new
 
 
 def rms_scale(values, gain_row):
@@ -137,7 +148,7 @@
         jnp.zeros((requests, KV_HEADS, 2), jnp.float32), own_den, row_first, 0
     )
     key_piece = lax.all_gather(prompt_keys, "grp", axis=0, tiled=True)
-    value_piece = lax.all_gather(prompt_values, "grp", axis=0, tiled=True)
+    value_piece = _change_levels_all(prompt_values, "grp")
     piece_rows = key_piece.shape[0]
     gathered_index = jnp.arange(piece_rows, dtype=jnp.int32)
     home_index = gathered_index // cap_dev

time: 626 us -> 599 us (0.957)
  waiting for transfers between devices: 419 us -> 385 us
  local copies, waits for them, and re-layouts: 23.3 us -> 32.7 us
  starting transfers between devices: 0.39 us -> 8.89 us
  matrix products: 28.5 us -> 21.3 us
    all_to_all x0 -> x1, waiting for transfers between devices: none -> 60.4 us  [_change_levels_all(): jax.lax.all_to_all(jnp.stack([base_x] * jax.lax.axis_size(which_axis)), c...]
    all_gather x1 -> x0, waiting for transfers between devices: 55.1 us -> none  [per_device(): value_piece = lax.all_gather(prompt_values, 'grp', axis=0, tiled=True)]
    all_gather x1, waiting for transfers between devices: 50.9 us -> 21.5 us  [per_device(): key_piece = lax.all_gather(prompt_keys, 'grp', axis=0, tiled=True)]
    all_gather x1, waiting for transfers between devices: 46.5 us -> 36.5 us  [per_device(): projected_qkv = lax.all_gather(qkv_share, 'tp', axis=1, tiled=True)]
    all_to_all x0 -> x1, starting transfers between devices: none -> 8.33 us  [_change_levels_all(): jax.lax.all_to_all(jnp.stack([base_x] * jax.lax.axis_size(which_axis)), c...]
    unnamed x35 -> x41, local copies, waits for them, and re-layouts: 9.03 us -> 16 us
    unnamed x8 -> x7, waiting for transfers between devices: 228 us -> 228 us
  transfers between devices with their start and end apart: 6 -> 6, of which waited for: 6 -> 6; matrix products, arithmetic and copies ran while one was open for 5% -> 6% of each run, Pallas kernels for 0% -> 0%
where the time goes in v1:
time: 599 us; the launch traced here: 598 us
  waiting for transfers between devices  385 us (64%)
  blocking collectives  119 us (20%)
  local copies, waits for them, and re-layouts  32.7 us (5%)
  matrix products  21.3 us (4%)
  other arithmetic  16.3 us (3%)
  between operations  14.1 us (2%)
  starting transfers between devices  8.89 us (1%)
    unnamed x7, waiting for transfers between devices  228 us
    psum x1, blocking collectives, per_device(): total_num, total_den = lax.psum((flat_num, flat_den), 'tp')  64.6 us
    all_to_all x1, waiting for transfers between devices, _change_levels_all(): jax.lax.all_to_all(jnp.stack([base_x] * jax.lax.axis_size(which_axis)), c...  60.4 us
    psum x1, waiting for transfers between devices, per_device(): total_num, total_den = lax.psum((flat_num, flat_den), 'tp')  38.5 us
    all_gather x1, waiting for transfers between devices, per_device(): projected_qkv = lax.all_gather(qkv_share, 'tp', axis=1, tiled=True)  36.5 us
    all_gather x1, blocking collectives, per_device(): lax.all_gather(ffn_in, 'tp', axis=0, tiled=True)  28.2 us
    all_gather x1, blocking collectives, per_device(): lax.all_gather(normed, 'tp', axis=0, tiled=True)  26.6 us
    all_gather x1, waiting for transfers between devices, per_device(): key_piece = lax.all_gather(prompt_keys, 'grp', axis=0, tiled=True)  21.5 us
  transfers between devices with their start and end apart: 6, of which 6 were waited for; matrix products, arithmetic and copies ran while one was open for 6% of the time, Pallas kernels for 0%

profile of v1, /device:TPU:1, one launch (start us, length us, event | category | flops | bytes accessed | tf_op | source)
XLA Modules:
  0.0 597.8 jit_solution(15450793808265596107)
XLA Ops:
  6.5 1.0 fusion.36
  7.6 1.1 slice_reduce_fusion.1
  8.7 0.8 fusion.48
  9.5 26.6 %all-gather = bf16[32,4,3584]{2,1,0:T(4,128)(2,1)S(1)} all-gather(bf16[1,4,3584]{2,1,0:T(4,128)(2,1)S(1)} %fusion.48), channel_id=1, replica_groups=mesh['grp'=8,'tp'=32] {'tp'}, dimensions={0}, use_global_device_ids=true | all-gather | bytes 946176 | tf_op jit(solution)/shard_map/all_gather | solution.py:114
  36.1 1.1 reshape.277
  37.2 2.8 convolution_convert_fusion.1
  40.1 2.5 stack.2
  42.7 8.3 %all-to-all-start = ((bf16[8,128,2048]{2,1,0:T(8,128)(2,1)}), bf16[8,128,2048]{2,1,0:T(8,128)(2,1)}, u32[]{:S(2)}, u32[]{:S(2)}) async-start(bf16[8,128,2048]{2,1,0:T(8,128)(2,1)} %stack.2), calls=%async_computation | async-start | bytes 8388608 | tf_op jit(solution)/shard_map/all_to_all | solution.py:15
  51.0 1.0 copy.73
  52.1 0.2 all-reduce.6.cloned.1.call-start
  52.3 0.1 dynamic_slice.12
  52.5 0.2 select_reduce_fusion.2
  52.6 0.1 select_reduce_fusion.3
  52.8 0.1 iota_compare_fusion.4
  52.8 0.3 multiply_cosine_fusion
  53.2 0.9 compare_and_fusion
  54.0 36.5 %all-gather.5.cloned.1.call-done = bf16[128,8192]{1,0:T(8,128)(2,1)} async-done(((bf16[128,256]{1,0:T(8,128)(2,1)}), bf16[128,8192]{1,0:T(8,128)(2,1)}) %all-gather.5.cloned.1.call-update) | async-done | bytes 2097168 | tf_op jit(solution)/shard_map/all_gather | solution.py:116
  90.5 1.4 slice_convert_fusion
  91.9 0.7 copy.96
  92.6 0.3 subtract_convert_fusion
  92.9 0.1 copy.71
  93.1 1.1 copy-done.3
  94.2 0.2 slice_convert_fusion.2
  94.4 1.3 copy.98
  95.7 1.4 copy.99
  97.1 0.1 copy.72
  97.3 0.5 fusion.74
  97.8 0.1 copy.83
  97.9 1.4 subtract_convert_fusion.1
  99.4 1.1 pad_maximum_fusion
  100.6 0.3 fusion.11
  100.8 60.4 %all-to-all-done = bf16[8,128,2048]{2,1,0:T(8,128)(2,1)} async-done(((bf16[8,128,2048]{2,1,0:T(8,128)(2,1)}), bf16[8,128,2048]{2,1,0:T(8,128)(2,1)}, u32[]{:S(2)}, u32[]{:S(2)}) %all-to-all-start) | async-done | bytes 4194336 | tf_op jit(solution)/shard_map/all_to_all | solution.py:15
  161.2 5.7 copy.97
  166.9 21.5 %all-gather.7.cloned.1.call-done = bf16[1024,2048]{0,1:T(8,128)(2,1)} async-done(((bf16[128,2048]{0,1:T(8,128)(2,1)}), bf16[1024,2048]{0,1:T(8,128)(2,1)}) %all-gather.7.cloned.1.call-update) | async-done | bytes 4194320 | tf_op jit(solution)/shard_map/all_gather | solution.py:150
  188.4 5.1 bitcast_reduce_fusion
  193.5 2.5 fusion
  196.0 1.4 copy.121
  197.3 0.7 fusion.29
  198.0 2.9 copy.80
  200.9 2.9 copy.81
  203.8 0.3 all-reduce.8.cloned.1.call-start
  204.1 3.3 fusion.16
  207.5 1.2 copy.89
  208.7 0.2 copy.82
  209.0 2.8 broadcast_multiply_fusion
  211.7 4.0 mul.269
  215.7 0.1 dynamic-slice_add_fusion
  215.8 1.3 add.147
  217.1 64.6 %psum.15 = f32[128,16]{0,1:T(8,128)S(1)} all-reduce(f32[128,16]{0,1:T(8,128)S(1)} %bitcast.94), channel_id=1, replica_groups=mesh['grp'=8,'tp'=32] {'tp'}, use_global_device_ids=true, to_apply=%region_8.9 | all-reduce | flops 2048 | bytes 16384 | tf_op jit(solution)/shard_map/psum | solution.py:172
  281.7 38.5 %all-reduce.6.cloned.1.call-done = f32[128,4096]{1,0:T(8,128)} async-done(((f32[128,4096]{1,0:T(8,128)}), f32[128,4096]{1,0:T(8,128)}) %all-reduce.6.cloned.1.call-update) | async-done | bytes 2097168 | tf_op jit(solution)/shard_map/psum | solution.py:172
  320.2 1.1 fusion.6
  321.4 1.6 fusion.75
  323.1 0.6 dynamic-slice.6
  324.4 115.3 %all-reduce.8.cloned.1.call-done = f32[128,3584]{1,0:T(8,128)} async-done(((f32[128,3584]{1,0:T(8,128)}), f32[128,3584]{1,0:T(8,128)}) %all-reduce.8.cloned.1.call-update) | async-done | bytes 1835024
  439.7 1.0 multiply_reduce_fusion
  440.7 1.1 fusion.40
  441.9 0.1 fusion.47
  442.0 28.2 %all-gather.1 = bf16[32,4,3584]{2,1,0:T(4,128)(2,1)} all-gather(bf16[1,4,3584]{2,1,0:T(4,128)(2,1)S(1)} %fusion.47), channel_id=1, replica_groups=mesh['grp'=8,'tp'=32] {'tp'}, dimensions={0}, use_global_device_ids=true | all-gather | bytes 946176 | tf_op jit(solution)/shard_map/all_gather | solution.py:204
  470.2 1.7 reshape.284
  471.8 2.7 convolution_bitcast_fusion
  474.5 1.4 convolution_convert_fusion
  476.0 112.7 %all-reduce.10.cloned.1.call-done = bf16[128,3584]{1,0:T(8,128)(2,1)} async-done(((bf16[128,3584]{1,0:T(8,128)(2,1)}), bf16[128,3584]{1,0:T(8,128)(2,1)}) %all-reduce.10.cloned.1.call-update) | async-done | bytes 917520
  588.7 1.0 fusion.34
  589.7 1.5 fusion.43
  (51 shorter events, 0.4 us)
Async XLA Ops:
  6.5 468.0 %copy-start = (bf16[256,3584]{1,0:T(8,128)(2,1)S(1)}, bf16[256,3584]{1,0:T(8,128)(2,1)}, u32[]{:S(2)}) copy-start(bf16[256,3584]{1,0:T(8,128)(2,1)} %param.19) | copy-start | bytes 5505028
  6.5 83.9 %all-gather.5.cloned.1.call-start = ((), (), s32[]{:S(2)}) async-start(), calls=%async_computation.1 | async-start | bytes 2162688 | tf_op jit(solution)/shard_map/all_gather | solution.py:116
  36.1 4.0 copy-start.6
  42.6 8.4 %copy-start.7 = (bf16[128,2048]{1,0:T(8,128)(2,1)S(1)}, bf16[128,2048]{1,0:T(8,128)(2,1)}, u32[]{:S(2)}) copy-start(bf16[128,2048]{1,0:T(8,128)(2,1)} %param.20) | copy-start | bytes 1572868
  42.6 9.7 %copy-start.13 = (s32[128]{0:T(128)S(1)}, s32[128]{0:T(128)}, u32[]{:S(2)}) copy-start(s32[128]{0:T(128)} %param.27) | copy-start | bytes 1540
  42.6 9.8 %copy-start.10 = (s32[80]{0:T(128)S(1)}, s32[80]{0:T(128)}, u32[]{:S(2)}) copy-start(s32[80]{0:T(128)} %param.25) | copy-start | bytes 964
  42.6 9.8 %copy-start.11 = (s32[80]{0:T(128)S(1)}, s32[80]{0:T(128)}, u32[]{:S(2)}) copy-start(s32[80]{0:T(128)} %param.24) | copy-start | bytes 964
  42.6 10.0 %copy-start.12 = (s32[128]{0:T(128)S(1)}, s32[128]{0:T(128)}, u32[]{:S(2)}) copy-start(s32[128]{0:T(128)} %param.26) | copy-start | bytes 1540
  42.7 118.5 %all-to-all-start = ((bf16[8,128,2048]{2,1,0:T(8,128)(2,1)}), bf16[8,128,2048]{2,1,0:T(8,128)(2,1)}, u32[]{:S(2)}, u32[]{:S(2)}) async-start(bf16[8,128,2048]{2,1,0:T(8,128)(2,1)} %stack.2), calls=%async_computation | async-start | bytes 8388608 | tf_op jit(solution)/shard_map/all_to_all | solution.py:15
  51.0 137.4 %all-gather.7.cloned.1.call-start = ((), (), s32[]{:S(2)}) async-start(), calls=%async_computation.2 | async-start | bytes 4718592 | tf_op jit(solution)/shard_map/all_gather | solution.py:150
  52.1 268.2 %all-reduce.6.cloned.1.call-start = ((), (), s32[]{:S(2)}) async-start(), calls=%async_computation.3 | async-start | bytes 4194304 | tf_op jit(solution)/shard_map/psum | solution.py:172
  92.6 1.6 copy-start.3
  95.7 1.6 copy-start.14
  97.9 2.6 copy-start.4
  188.4 5.1 copy-start.2
  188.4 5.1 copy-start.9
  203.8 5.1 copy-start.1
  203.8 235.8 %all-reduce.8.cloned.1.call-start = ((), (), s32[]{:S(2)}) async-start(), calls=%async_computation.4 | async-start | bytes 3670016
  211.7 109.7 %copy-start.5 = (bf16[128,3584]{1,0:T(8,128)(2,1)S(1)}, bf16[128,3584]{1,0:T(8,128)(2,1)}, u32[]{:S(2)}) copy-start(bf16[128,3584]{1,0:T(8,128)(2,1)} %param.17) | copy-start | bytes 2752516
  321.4 1.7 copy-start.15
  321.4 119.3 %copy-start.8 = (bf16[4,3584]{1,0:T(4,128)(2,1)S(1)}, bf16[4,3584]{1,0:T(4,128)(2,1)}, u32[]{:S(2)}) copy-start(bf16[4,3584]{1,0:T(4,128)(2,1)} %param.14) | copy-start | bytes 86020
  323.1 265.7 %all-reduce.10.cloned.1.call-start = ((), (), s32[]{:S(2)}) async-start(), calls=%async_computation.5 | async-start | bytes 1835008
Sparse Core Ops, SparseCore 0:
  40.2 50.2 all-gather.4
  92.2 96.1 all-gather.6
  204.0 116.2 all-reduce.5
  323.4 116.2 all-reduce.7
  476.1 112.5 all-reduce.9
